TPU v7x, 32 devices: a whole 2x2x4 slice. The times are simulated.
32 devices in a mesh: tgt: 2 (over core), sup: 16 (over z, y, x).
Axes of the slice: x: 2, y: 2, z: 4, core: 2. Of those that a mesh axis runs over, the one named last changes fastest.
Arguments:
- image_pool: bfloat16 [2048, 3072], P(('tgt', 'sup')), may hold values from -1 to 2
- target_index: int32 [64], replicated, may hold values from 0 to 2047, as said below
- labels: int32 [64], P('tgt'), may hold values from 0 to 1023
- support: float32 [64, 3, 1024], P('sup'), may hold values from -1 to 2
- ridge_coef: float32 [64, 1024], P('sup'), may hold values from -1.5 to 1.5
Outputs:
- residual: float32 [64, 1024], P('tgt', 'sup')
- support_grad: float32 [64, 3, 1024], P('sup')
Inputs may be any that keep to these rules, and one draw needn't show every extreme that they name: `target_index`: any row of the pool; the first of each group's 32 targets lies in the pool rows of the devices half the tgt axis away.
All inputs are finite; a program needn't handle non-finite values.
Results may differ from a plain program's by a relative error of at most 0.0003.
Values may be sent and summed in bfloat16 or wider, within the bound.
A program may use at most 64 MiB of HBM per device.

v0:
```python
import math
import jax
import jax.numpy as jnp
from jax import lax
from jax.sharding import PartitionSpec as P

SIDE = 32
CHAN = 3
LAYERS = 4
WEIGHT_VAR = 2.0
BIAS_VAR = 0.1


def box_sum(values_map):
    column = jnp.arange(SIDE * SIDE) % SIDE
    zero_col = jnp.zeros(values_map.shape[:-1] + (1,), values_map.dtype)
    from_left = jnp.concatenate([zero_col, values_map[..., :-1]], -1)
    from_right = jnp.concatenate([values_map[..., 1:], zero_col], -1)
    row_sum = (
        values_map
        + jnp.where(column > 0, from_left, 0.0)
        + jnp.where(column < SIDE - 1, from_right, 0.0)
    )
    zero_row = jnp.zeros(values_map.shape[:-1] + (SIDE,), values_map.dtype)
    from_above = jnp.concatenate([zero_row, row_sum[..., :-SIDE]], -1)
    from_below = jnp.concatenate([row_sum[..., SIDE:], zero_row], -1)
    return (row_sum + from_above + from_below) / 9.0


def self_maps(pixels):
    current = jnp.sum(pixels * pixels, axis=1) / 3.0
    variances = []
    for depth in range(LAYERS):
        variance = WEIGHT_VAR * box_sum(current) + BIAS_VAR
        variances.append(variance)
        current = 2.0 / math.pi * jnp.arcsin(2.0 * variance / (1.0 + 2.0 * variance))
    return variances


def cross_layer(current, target_var, support_var):
    covariance = WEIGHT_VAR * box_sum(current) + BIAS_VAR
    denominator = jnp.sqrt(
        (1.0 + 2.0 * target_var)[:, None, :] * (1.0 + 2.0 * support_var)[None, :, :]
    )
    return 2.0 / math.pi * jnp.arcsin(2.0 * covariance / denominator)


def kernel_rows(targets, support, layer_step):
    target_vars = self_maps(targets)
    support_vars = self_maps(support)
    current = jnp.einsum("icp,jcp->ijp", targets, support, precision=lax.Precision.HIGHEST) / 3.0
    for depth in range(LAYERS):
        current = layer_step(current, target_vars[depth], support_vars[depth])
    return jnp.mean(current, axis=-1)


def local(image_pool, target_index, labels, support, ridge_coef):
    pool_rows = image_pool.shape[0]
    tgt_dev = labels.shape[0]
    flat_rank = lax.axis_index("tgt") * lax.axis_size("sup") + lax.axis_index("sup")
    owned_ids = flat_rank * pool_rows + jnp.arange(pool_rows, dtype=jnp.int32)
    selector = (target_index[:, None] == owned_ids[None, :]).astype(jnp.bfloat16)
    picked = jnp.dot(selector, image_pool, preferred_element_type=jnp.float32)
    every_target = lax.psum(picked, ("tgt", "sup"))
    group_pixels = lax.dynamic_slice_in_dim(
        every_target, lax.axis_index("tgt") * tgt_dev, tgt_dev, 0
    )
    targets = group_pixels.reshape(tgt_dev, CHAN, -1)
    layer_step = jax.checkpoint(cross_layer)
    kernel_block, pullback = jax.vjp(
        lambda points: kernel_rows(targets, points, layer_step), support
    )
    partial_value = jnp.dot(
        kernel_block,
        ridge_coef,
        precision=lax.Precision.HIGHEST,
        preferred_element_type=jnp.float32,
    )
    n_classes = ridge_coef.shape[1]
    per_owner = n_classes // lax.axis_size("sup")
    mine_pred = lax.psum_scatter(partial_value, "sup", scatter_dimension=1, tiled=True)
    class_start = lax.axis_index("sup") * per_owner
    target_hot = (
        labels[:, None] == class_start + jnp.arange(per_owner, dtype=jnp.int32)[None, :]
    ).astype(jnp.float32)
    residual = mine_pred - target_hot
    full_residual = lax.all_gather(residual, "sup", axis=1, tiled=True)
    loss_scale = float(SIDE * SIDE) / tgt_dev
    kernel_grad = loss_scale * jnp.dot(
        full_residual,
        ridge_coef.T,
        precision=lax.Precision.HIGHEST,
        preferred_element_type=jnp.float32,
    )
    local_grad = pullback(kernel_grad)[0]
    support_grad = lax.psum(local_grad, "tgt")
    return (residual, support_grad)


def solution(mesh):
    in_specs = (P(("tgt", "sup"), None), P(), P("tgt"), P("sup", None, None), P("sup", None))
    out_specs = (P("tgt", "sup"), P("sup", None, None))
    return jax.shard_map(local, mesh=mesh, in_specs=in_specs, out_specs=out_specs, check_vma=False)
```

profile of v0, /device:TPU:0, one launch (start us, length us, event | category | flops | bytes accessed | tf_op | source)
XLA Modules:
  0.0 323.5 jit_solution(5069627839205184832)
XLA Ops:
  7.3 0.9 copy-done
  8.2 1.8 fusion
  10.1 2.5 copy.79
  14.2 131.6 %all-reduce.98.cloned.1.call-done = f32[64,3072]{1,0:T(8,128)} async-done(((f32[64,3072]{1,0:T(8,128)}), f32[64,3072]{1,0:T(8,128)}) %all-reduce.98.cloned.1.call-update) | async-done | bytes 786448 | tf_op jit(solution)/shard_map/psum | solution.py:64
  145.8 1.0 constant_dynamic-slice_fusion
  146.9 0.3 reshape.46
  147.2 0.9 copy.78
  148.1 0.3 multiply_reduce_fusion.5
  148.4 9.9 %fusion.55 = f32[1024,32,4]{1,2,0:T(4,128)} fusion(f32[32,3,1024]{0,1,2:T(4,128)S(1)} %copy.78, f32[4,3,1024]{1,0,2:T(4,128)} %copy.79), kind=kOutput, calls=%fused_computation.181 | convolution fusion | flops 4718592 | bytes 966656 | tf_op jit(solution)/shard_map/jvp(icp,jcp->ijp)/dot_general | solution.py:51
  158.3 2.0 copy.80
  161.3 0.4 add_multiply_fusion.9
  161.8 0.3 select_add_fusion.10
  162.1 1.2 add_multiply_fusion.6
  163.6 0.2 select_add_fusion.6
  164.1 0.4 add_multiply_fusion.8
  164.6 0.3 select_add_fusion.9
  164.9 1.2 add_multiply_fusion.5
  166.3 0.2 select_add_fusion.5
  166.8 0.4 add_multiply_fusion.7
  167.3 0.3 select_add_fusion.8
  167.7 1.2 add_multiply_fusion.4
  169.1 0.2 select_add_fusion.4
  169.8 1.3 multiply_reduce_fusion.4
  171.1 1.8 convolution_bitcast_fusion
  173.0 76.7 %reduce-scatter.4.cloned.1.call-done = f32[64,32]{1,0:T(8,128)} async-done(((f32[1024,32]{1,0:T(8,128)}), f32[64,32]{1,0:T(8,128)}) %reduce-scatter.4.cloned.1.call-update) | async-done | bytes 8208
  249.7 0.8 copy.95
  250.5 0.7 convert_subtract_fusion
  251.3 37.5 %all-gather = f32[16,64,32]{1,2,0:T(8,128)S(1)} all-gather(f32[1,64,32]{1,2,0:T(8,128)S(1)} %fusion.65), channel_id=1, replica_groups=mesh['tgt'=2,'sup'=16] {'sup'}, dimensions={0}, use_global_device_ids=true | all-gather | bytes 139264 | tf_op jit(solution)/shard_map/all_gather | solution.py:87
  289.6 0.2 select_add_fusion.3
  290.0 0.7 multiply_reduce_fusion
  290.9 0.2 pad_add_fusion.6
  291.1 0.2 slice_select_fusion.7
  291.8 0.2 select_add_fusion.2
  292.2 0.7 multiply_reduce_fusion.1
  293.1 0.2 pad_add_fusion.4
  293.3 0.2 slice_select_fusion.5
  294.0 0.2 select_add_fusion.1
  294.4 0.7 multiply_reduce_fusion.2
  295.2 0.2 pad_add_fusion.2
  295.5 0.2 slice_select_fusion.3
  296.1 0.2 select_add_fusion
  296.5 0.7 multiply_reduce_fusion.3
  297.4 0.2 pad_add_fusion
  297.6 0.2 slice_select_fusion.1
  298.1 2.0 copy.83
  300.1 9.4 %fusion.56 = f32[1024,4,3]{1,2,0:T(4,128)} fusion(f32[1024,4,32]{2,1,0:T(4,128)} %copy.83, f32[32,3,1024]{0,1,2:T(4,128)S(1)} %copy-done.2), kind=kOutput, calls=%fused_computation.182 | convolution fusion | flops 4718592 | bytes 966656 | tf_op jit(solution)/shard_map/transpose(jvp(icp,jcp->ijp))/dot_general | solution.py:51
  309.4 1.8 copy.85
  312.6 4.1 %psum.15 = f32[4,3,1024]{2,0,1:T(4,128)} all-reduce(f32[4,3,1024]{2,0,1:T(4,128)S(1)} %add_add_fusion), channel_id=1, replica_groups=mesh['tgt'=2,'sup'=16] {'tgt'}, use_global_device_ids=true, to_apply=%region_9.10 | all-reduce | flops 12288 | bytes 98304 | tf_op jit(solution)/shard_map/psum | solution.py:96
  (108 shorter events, 10.0 us)
Async XLA Ops:
  7.2 1.0 copy-start
  7.2 5.4 %copy-start.3 = (f32[4,3,1024]{2,0,1:T(4,128)S(1)}, f32[4,3,1024]{2,0,1:T(4,128)}, u32[]{:S(2)}) copy-start(f32[4,3,1024]{2,0,1:T(4,128)} %param.8) | copy-start | bytes 147460
  7.2 138.6 %all-reduce.98.cloned.1.call-start = ((), (), s32[]{:S(2)}) async-start(), calls=%async_computation.1 | async-start | bytes 1572864 | tf_op jit(solution)/shard_map/psum | solution.py:64
  10.0 239.7 %reduce-scatter.4.cloned.1.call-start = ((), (), s32[]{:S(2)}) async-start(), calls=%async_computation.2 | async-start | bytes 557056
  148.0 10.2 %copy-start.1 = (f32[32,3,1024]{0,1,2:T(4,128)}, f32[32,3,1024]{0,1,2:T(4,128)S(1)}, u32[]{:S(2)}) copy-start(f32[32,3,1024]{0,1,2:T(4,128)S(1)} %copy.78) | copy-start | bytes 1179652
  169.3 1.8 copy-start.4
  169.5 81.0 %copy-start.5 = (s32[32]{0:T(128)S(1)}, s32[32]{0:T(128)}, u32[]{:S(2)}) copy-start(s32[32]{0:T(128)} %param.7) | copy-start | bytes 388
  297.9 2.2 copy-start.2
Sparse Core Ops, SparseCore 0:
  13.2 132.6 all-reduce.97
  173.1 76.5 reduce-scatter.3
where the time goes:
time: 324 us
  waiting for transfers between devices  208 us (64%)
  blocking collectives  41.6 us (13%)
  matrix products  23 us (7%)
  local copies, waits for them, and re-layouts  18.4 us (6%)
  other arithmetic  17.5 us (5%)
  between operations  14.6 us (5%)
    psum x1, waiting for transfers between devices, local(): every_target = lax.psum(picked, ('tgt', 'sup'))  132 us
    unnamed x3, waiting for transfers between devices  76.7 us
    all_gather x1, blocking collectives, local(): full_residual = lax.all_gather(residual, 'sup', axis=1, tiled=True)  37.5 us
    dot_general x2, matrix products, kernel_rows(): jnp.einsum('icp,jcp->ijp', targets, support, precision=lax.Precision.HIGH...  19.2 us
  transfers between devices with their start and end apart: 2, of which 2 were waited for; matrix products, arithmetic and copies ran while one was open for 1% of the time, Pallas kernels for 0%

commit v1 on v0

--- a/solution.py
+++ b/solution.py
@@ -61,7 +61,7 @@
     owned_ids = flat_rank * pool_rows + jnp.arange(pool_rows, dtype=jnp.int32)
     selector = (target_index[:, None] == owned_ids[None, :]).astype(jnp.bfloat16)
     picked = jnp.dot(selector, image_pool, preferred_element_type=jnp.float32)
-    every_target = lax.psum(picked, ("tgt", "sup"))
+    every_target = jnp.sum(lax.all_gather(picked, ("tgt", "sup")), axis=0)
     group_pixels = lax.dynamic_slice_in_dim(
         every_target, lax.axis_index("tgt") * tgt_dev, tgt_dev, 0
     )

time: 324 us -> 360 us (1.11)
  waiting for transfers between devices: 208 us -> 227 us
  other arithmetic: 17.5 us -> 32.3 us
  local copies, waits for them, and re-layouts: 18.4 us -> 22.3 us
    all_gather x0 -> x1, waiting for transfers between devices: none -> 151 us  [local(): every_target = jnp.sum(lax.all_gather(picked, ('tgt', 'sup')), axis=0)]
    psum x1 -> x0, waiting for transfers between devices: 132 us -> none  [local(): every_target = lax.psum(picked, ('tgt', 'sup'))]
    reduce_sum x0 -> x1, other arithmetic: none -> 9.2 us  [local(): every_target = jnp.sum(lax.all_gather(picked, ('tgt', 'sup')), axis=0)]
    unnamed x15 -> x61, local copies, waits for them, and re-layouts: 4.36 us -> 7.87 us
  transfers between devices with their start and end apart: 2 -> 2, of which waited for: 2 -> 2; matrix products, arithmetic and copies ran while one was open for 1% -> 2% of each run, Pallas kernels for 0% -> 0%
where the time goes in v1:
time: 360 us
  waiting for transfers between devices  227 us (63%)
  blocking collectives  41.8 us (12%)
  other arithmetic  32.3 us (9%)
  local copies, waits for them, and re-layouts  22.3 us (6%)
  matrix products  21.5 us (6%)
  between operations  14.7 us (4%)
    all_gather x1, waiting for transfers between devices, local(): every_target = jnp.sum(lax.all_gather(picked, ('tgt', 'sup')), axis=0)  151 us
    unnamed x3, waiting for transfers between devices  75.9 us
    all_gather x1, blocking collectives, local(): full_residual = lax.all_gather(residual, 'sup', axis=1, tiled=True)  37.7 us
    dot_general x2, matrix products, kernel_rows(): jnp.einsum('icp,jcp->ijp', targets, support, precision=lax.Precision.HIGH...  17.7 us
    reduce_sum x1, other arithmetic, local(): every_target = jnp.sum(lax.all_gather(picked, ('tgt', 'sup')), axis=0)  9.2 us
    unnamed x61, local copies, waits for them, and re-layouts  7.87 us
  transfers between devices with their start and end apart: 2, of which 2 were waited for; matrix products, arithmetic and copies ran while one was open for 2% of the time, Pallas kernels for 0%

profile of v1, /device:TPU:0, one launch (start us, length us, event | category | flops | bytes accessed | tf_op | source)
XLA Modules:
  0.0 359.5 jit_solution(7315359637862583473)
XLA Ops:
  7.3 0.9 copy-done
  8.2 1.8 fusion
  10.1 2.5 copy.79
  13.9 0.6 multiply_add_fusion.21
  14.5 0.6 multiply_add_fusion.23
  15.1 0.6 multiply_add_fusion.22
  15.9 0.7 multiply_add_fusion.16
  16.6 151.0 %all-gather.4.cloned.1.call-done = f32[2048,3072]{1,0:T(8,128)} async-done(((f32[64,3072]{1,0:T(8,128)}), f32[2048,3072]{1,0:T(8,128)}) %all-gather.4.cloned.1.call-update) | async-done | bytes 25165840 | tf_op jit(solution)/shard_map/all_gather | solution.py:64
  167.7 9.2 %reduce_sum.70 = f32[64,3072]{1,0:T(8,128)S(1)} reduce(f32[32,64,3072]{2,1,0:T(8,128)} %bitcast.27, f32[]{:T(128)} %constant.190.clone.1), dimensions={0}, to_apply=%region_0.0 | reduce | flops 6094848 | bytes 25952260 | tf_op jit(solution)/shard_map/reduce_sum | solution.py:64
  176.9 0.3 reshape.46
  177.2 0.3 multiply_reduce_fusion.5
  177.6 0.9 copy.78
  178.8 0.4 add_multiply_fusion.9
  179.3 0.9 select_add_fusion.10
  180.3 0.4 add_multiply_fusion.8
  180.8 0.9 select_add_fusion.9
  181.8 0.4 add_multiply_fusion.7
  182.3 0.9 select_add_fusion.8
  183.3 0.8 fusion.35
  184.0 8.2 %fusion.55 = f32[1024,32,4]{1,2,0:T(4,128)} fusion(f32[32,3,1024]{0,1,2:T(4,128)S(1)} %copy.78, f32[4,3,1024]{1,0,2:T(4,128)S(1)} %copy-done.4), kind=kOutput, calls=%fused_computation.181 | convolution fusion | flops 4718592 | bytes 966656 | tf_op jit(solution)/shard_map/jvp(icp,jcp->ijp)/dot_general | solution.py:51
  192.3 2.0 copy.80
  195.0 0.5 copy-done.7
  195.5 1.2 add_multiply_fusion.6
  197.3 0.5 copy-done.8
  197.8 1.2 add_multiply_fusion.5
  199.7 0.5 copy-done.9
  200.2 1.2 add_multiply_fusion.4
  202.0 0.4 copy-done.11
  202.5 0.8 multiply_add_fusion.4
  203.3 1.3 multiply_reduce_fusion.4
  204.7 1.8 convolution_bitcast_fusion
  206.6 75.8 %reduce-scatter.4.cloned.1.call-done = f32[64,32]{1,0:T(8,128)} async-done(((f32[1024,32]{1,0:T(8,128)}), f32[64,32]{1,0:T(8,128)}) %reduce-scatter.4.cloned.1.call-update) | async-done | bytes 8208
  282.4 0.8 copy.95
  283.3 0.7 convert_subtract_fusion
  284.0 37.7 %all-gather.1 = f32[16,64,32]{1,2,0:T(8,128)S(1)} all-gather(f32[1,64,32]{1,2,0:T(8,128)S(1)} %fusion.65), channel_id=1, replica_groups=mesh['tgt'=2,'sup'=16] {'sup'}, dimensions={0}, use_global_device_ids=true | all-gather | bytes 139264 | tf_op jit(solution)/shard_map/all_gather | solution.py:87
  322.9 0.5 copy-done.10
  323.4 0.7 multiply_reduce_fusion
  325.9 0.5 copy-done.6
  326.4 0.7 multiply_reduce_fusion.1
  328.9 0.3 copy-done.18
  329.2 0.7 multiply_reduce_fusion.2
  331.6 0.3 copy-done.16
  331.9 0.7 multiply_reduce_fusion.3
  333.6 1.0 multiply_bitcast_fusion
  334.6 2.6 copy.83
  337.2 9.4 %fusion.56 = f32[1024,4,3]{1,2,0:T(4,128)} fusion(f32[1024,4,32]{2,1,0:T(4,128)} %copy.83, f32[32,3,1024]{0,1,2:T(4,128)S(1)} %copy-done.3), kind=kOutput, calls=%fused_computation.182 | convolution fusion | flops 4718592 | bytes 966656 | tf_op jit(solution)/shard_map/transpose(jvp(icp,jcp->ijp))/dot_general | solution.py:51
  346.7 1.8 copy.85
  348.6 4.1 %psum.7 = f32[4,3,1024]{2,0,1:T(4,128)} all-reduce(f32[4,3,1024]{2,0,1:T(4,128)S(1)} %add_add_fusion), channel_id=1, replica_groups=mesh['tgt'=2,'sup'=16] {'tgt'}, use_global_device_ids=true, to_apply=%region_9.10 | all-reduce | flops 12288 | bytes 98304 | tf_op jit(solution)/shard_map/psum | solution.py:96
  (155 shorter events, 12.8 us)
Async XLA Ops:
  7.2 1.0 copy-start
  7.2 5.4 %copy-start.13 = (f32[4,3,1024]{2,0,1:T(4,128)S(1)}, f32[4,3,1024]{2,0,1:T(4,128)}, u32[]{:S(2)}) copy-start(f32[4,3,1024]{2,0,1:T(4,128)} %param.8) | copy-start | bytes 147460
  7.2 160.5 %all-gather.4.cloned.1.call-start = ((), (), s32[]{:S(2)}) async-start(), calls=%async_computation.1 | async-start | bytes 25952256 | tf_op jit(solution)/shard_map/all_gather | solution.py:64
  10.0 272.4 %reduce-scatter.4.cloned.1.call-start = ((), (), s32[]{:S(2)}) async-start(), calls=%async_computation.2 | async-start | bytes 557056
  13.0 154.7 %copy-start.15 = (f32[4,1024]{1,0:T(4,128)}, f32[4,1024]{1,0:T(4,128)S(1)}, u32[]{:S(2)}) copy-start(f32[4,1024]{1,0:T(4,128)S(1)} %get-tuple-element.33) | copy-start | bytes 49156
  13.4 154.2 %copy-start.17 = (f32[4,1024]{1,0:T(4,128)}, f32[4,1024]{1,0:T(4,128)S(1)}, u32[]{:S(2)}) copy-start(f32[4,1024]{1,0:T(4,128)S(1)} %get-tuple-element.29) | copy-start | bytes 49156
  13.9 153.8 %copy-start.19 = (f32[4,1024]{1,0:T(4,128)}, f32[4,1024]{1,0:T(4,128)S(1)}, u32[]{:S(2)}) copy-start(f32[4,1024]{1,0:T(4,128)S(1)} %get-tuple-element.25) | copy-start | bytes 49156
  178.4 5.6 %copy-start.2 = (f32[32,3,1024]{0,1,2:T(4,128)}, f32[32,3,1024]{0,1,2:T(4,128)S(1)}, u32[]{:S(2)}) copy-start(f32[32,3,1024]{0,1,2:T(4,128)S(1)} %copy.78) | copy-start | bytes 1179652
  180.7 3.3 copy-start.4
  182.2 10.0 %copy-start.5 = (f32[32,1024]{1,0:T(8,128)}, f32[32,1024]{1,0:T(8,128)S(1)}, u32[]{:S(2)}) copy-start(f32[32,1024]{1,0:T(8,128)S(1)} %get-tuple-element.24) | copy-start | bytes 393220
  194.6 0.9 copy-start.7
  194.6 0.9 copy-start.24
  196.9 0.9 copy-start.8
  196.9 0.9 copy-start.23
  199.2 0.9 copy-start.9
  199.2 0.9 copy-start.22
  201.6 0.9 copy-start.11
  201.6 1.0 copy-start.12
  201.6 1.7 copy-start.21
  201.8 2.8 copy-start.25
  202.0 81.2 %copy-start.28 = (s32[32]{0:T(128)S(1)}, s32[32]{0:T(128)}, u32[]{:S(2)}) copy-start(s32[32]{0:T(128)} %param.7) | copy-start | bytes 388
  203.3 118.6 %copy-start.26 = (f32[4,1024]{1,0:T(4,128)S(1)}, f32[4,1024]{1,0:T(4,128)}, u32[]{:S(2)}) copy-start(f32[4,1024]{1,0:T(4,128)} %param.9) | copy-start | bytes 49156
  322.5 0.9 copy-start.10
  322.5 0.9 copy-start.27
  325.4 0.9 copy-start.6
  325.4 0.9 copy-start.20
  328.4 0.7 copy-start.18
  331.2 0.7 copy-start.16
  333.6 3.7 %copy-start.3 = (f32[32,3,1024]{0,1,2:T(4,128)S(1)}, f32[32,3,1024]{0,1,2:T(4,128)}, u32[]{:S(2)}) copy-start(f32[32,3,1024]{0,1,2:T(4,128)} %copy-done.2) | copy-start | bytes 1179652
  337.2 15.5 %copy-start.1 = (bf16[64,3072]{1,0:T(8,128)(2,1)S(1)}, bf16[64,3072]{1,0:T(8,128)(2,1)}, u32[]{:S(2)}) copy-start(bf16[64,3072]{1,0:T(8,128)(2,1)} %param.5) | copy-start | bytes 1179652
  346.7 1.9 copy-start.14
Sparse Core Ops, SparseCore 0:
  10.9 156.7 all-gather.3
  206.6 75.7 reduce-scatter.3
